TPU v7x, 32 devices: a whole 2x2x4 slice. The times are simulated.
32 devices in a mesh: row: 4 (over y, x), col: 8 (over z, core).
Axes of the slice: x: 2, y: 2, z: 4, core: 2. Of those that a mesh axis runs over, the one named last changes fastest.
Arguments:
- anc_inverse: float32 [10240, 10240], P('row', 'col'), may hold values from -0.0625 to 0.0625
- lower_anc: float32 [10240, 3, 384], P('col', None, 'row'), may hold values from -1.5 to 1.5
- upper_anc: float32 [10240, 3, 384], P('row', None, 'col'), may hold values from -0.75 to 0.75
- lower_edge: float32 [2, 384, 384], replicated, may hold values from -0.3125 to 0.3125
- upper_edge: float32 [2, 384, 384], replicated, may hold values from -0.3125 to 0.3125
- diag_inverse: float32 [3, 384, 384], replicated, may hold values from -6 to 6
- tile_mask: int32 [3, 80, 3], replicated, may hold values 0 or 1
Outputs:
- x_blocks: float32 [10240, 3, 384], P(('row', 'col'))
- y_blocks: float32 [8, 4, 320, 3, 384], P('col', 'row')
- z_blocks: float32 [3, 384, 384], P(None, 'row', 'col')
- cross_blocks: float32 [2, 2, 384, 384], P(None, None, 'row', 'col')
All inputs are finite; a program needn't handle non-finite values.
Results may differ from a plain program's by a relative error of at most 0.0001.
Values sent between devices are 32-bit elements; how exact they have to be, the bound alone decides.
A program may use at most 128 MiB of HBM per device.

v0:
```python
import jax
import jax.numpy as jnp
from jax import lax
from jax.sharding import PartitionSpec as P

W = 384
BLK = 128
SUPER = 3
precise = lax.Precision.HIGHEST


def product(left, right):
    return jnp.dot(left, right, precision=precise, preferred_element_type=jnp.float32)


def inner_product(left, right):
    return lax.dot_general(
        left, right, (((0,), (0,)), ((), ())), precision=precise, preferred_element_type=jnp.float32
    )


def outer_product(left, right):
    return lax.dot_general(
        left, right, (((1,), (1,)), ((), ())), precision=precise, preferred_element_type=jnp.float32
    )


def tile_pattern(tile_mask, first_block, blocks):
    window = lax.dynamic_slice_in_dim(tile_mask, first_block, blocks, 1).astype(jnp.float32)
    window = jnp.transpose(window, (1, 0, 2))
    widened = jnp.broadcast_to(window[:, None, :, :, None], (blocks, BLK, SUPER, W // BLK, BLK))
    return widened.reshape(blocks * BLK, SUPER, W)


def row_term(anc_inverse, lower_cols):
    return product(anc_inverse, lower_cols)


def col_term(anc_inverse, upper_rows):
    return inner_product(anc_inverse, upper_rows)


def per_device(anc_inverse, lower_anc, upper_anc, lower_edge, upper_edge, diag_inverse, tile_mask):
    rows_here, cols_here = anc_inverse.shape
    slab_rows = rows_here // lax.axis_size("col")
    row_index = lax.axis_index("row")
    col_index = lax.axis_index("col")
    col_pattern = tile_pattern(tile_mask, col_index * (cols_here // BLK), cols_here // BLK)
    row_pattern = tile_pattern(tile_mask, row_index * (rows_here // BLK), rows_here // BLK)
    lower_list = []
    upper_list = []
    cols_list = []
    rows_list = []
    lower_full = lax.all_gather(lower_anc, "row", axis=2, tiled=True) * col_pattern
    upper_full = lax.all_gather(upper_anc, "col", axis=2, tiled=True) * row_pattern
    cols_all = lax.psum_scatter(
        row_term(anc_inverse, lower_full.reshape(cols_here, SUPER * W)),
        "col",
        scatter_dimension=0,
        tiled=True,
    )
    rows_all = lax.psum_scatter(
        col_term(anc_inverse, upper_full.reshape(rows_here, SUPER * W)),
        "row",
        scatter_dimension=0,
        tiled=True,
    )
    cols_all = cols_all.reshape(slab_rows, SUPER, W)
    rows_all = rows_all.reshape(slab_rows, SUPER, W)
    for node_index in range(SUPER):
        lower_list.append(lower_full[:, node_index, :])
        upper_list.append(upper_full[:, node_index, :])
        cols_list.append(cols_all[:, node_index, :])
        rows_list.append(rows_all[:, node_index, :])
    x_list = []
    y_list = []
    corner_list = []
    cross_cols = []
    cross_rows = []
    for node_index in range(SUPER):
        lower_cur = lower_list[node_index]
        upper_cur = upper_list[node_index]
        inv_cols = -cols_list[node_index]
        inv_rows = -rows_list[node_index]
        upper_mine = lax.dynamic_slice_in_dim(upper_cur, col_index * slab_rows, slab_rows, 0)
        if node_index > 0:
            lower_side = lower_edge[node_index - 1]
            upper_side = upper_edge[node_index - 1]
            lower_mine = lax.dynamic_slice_in_dim(lower_cur, row_index * slab_rows, slab_rows, 0)
            rows_lower = inner_product(prev_rows, lower_mine)
            upper_cols = inner_product(upper_mine, prev_cols)
        if node_index > 0:
            rows_lower, upper_cols = lax.psum((rows_lower, upper_cols), ("row", "col"))
        if node_index > 0:
            cross_col = -(rows_lower + product(prev_corner, lower_side))
            cross_row = -(upper_cols + product(upper_side, prev_corner))
            inv_cols = inv_cols - product(prev_cols, lower_side)
            inv_rows = inv_rows - outer_product(prev_rows, upper_side)
            cross_cols.append(cross_col)
            cross_rows.append(cross_row)
        inv_corner = diag_inverse[node_index] - lax.psum(
            inner_product(upper_mine, inv_cols), ("row", "col")
        )
        if node_index > 0:
            inv_corner = inv_corner - product(upper_side, cross_col)
        x_list.append(inv_cols)
        y_list.append(inv_rows)
        corner_list.append(inv_corner)
        prev_cols = inv_cols
        prev_rows = inv_rows
        prev_corner = inv_corner
    x_blocks = jnp.stack(x_list, axis=1)
    y_blocks = jnp.stack(y_list, axis=1)[None, None]
    tile_rows = W // lax.axis_size("row")
    tile_cols = W // lax.axis_size("col")
    corners = jnp.stack(corner_list)
    corners = lax.dynamic_slice_in_dim(corners, row_index * tile_rows, tile_rows, 1)
    z_blocks = lax.dynamic_slice_in_dim(corners, col_index * tile_cols, tile_cols, 2)
    crossed = jnp.stack([jnp.stack(cross_cols), jnp.stack(cross_rows)])
    crossed = lax.dynamic_slice_in_dim(crossed, row_index * tile_rows, tile_rows, 2)
    cross_blocks = lax.dynamic_slice_in_dim(crossed, col_index * tile_cols, tile_cols, 3)
    return (x_blocks, y_blocks, z_blocks, cross_blocks)


def solution(mesh):
    return jax.shard_map(
        per_device,
        mesh=mesh,
        in_specs=(
            P("row", "col"),
            P("col", None, "row"),
            P("row", None, "col"),
            P(),
            P(),
            P(),
            P(),
        ),
        out_specs=(
            P(("row", "col"), None, None),
            P("col", "row", None, None, None),
            P(None, "row", "col"),
            P(None, None, "row", "col"),
        ),
        check_vma=False,
    )
```

profile of v0, /device:TPU:0, one launch (start us, length us, event | category | flops | bytes accessed | tf_op | source)
XLA Modules:
  0.0 565.6 jit_solution(17613502817447202190)
XLA Ops:
  8.9 4.2 broadcast_in_dim.6
  13.1 10.5 %reshape.42 = f32[1280,3,384]{2,0,1:T(8,128)} reshape(f32[10,128,3,3,128]{4,3,1,0,2:T(4,128)} %broadcast_in_dim.6) | data formatting | bytes 11796480 | tf_op jit(solution)/shard_map/reshape | solution.py:32
  23.6 55.8 %all-gather.3.cloned.1.call-done = f32[1280,3,384]{0,2,1:T(8,128)} async-done(((f32[1280,3,96]{0,2,1:T(8,128)}), f32[1280,3,384]{0,2,1:T(8,128)}) %all-gather.3.cloned.1.call-update) | async-done | bytes 5898256 | tf_op jit(solution)/shard_map/all_gather | solution.py:54
  79.3 7.7 %copy.70 = f32[1280,3,384]{2,0,1:T(8,128)} copy(f32[1280,3,384]{0,2,1:T(8,128)} %all-gather.3.cloned.1.call-done) | data formatting | bytes 11796480 | tf_op jit(solution)/shard_map/all_gather | solution.py:54
  87.0 9.3 %mul.30 = f32[1280,3,384]{2,0,1:T(8,128)} multiply(f32[1280,3,384]{2,0,1:T(8,128)} %copy.70, f32[1280,3,384]{2,0,1:T(8,128)} %reshape.42) | non-fusion elementwise | flops 1474560 | bytes 17694720 | tf_op jit(solution)/shard_map/mul | solution.py:54
  96.3 7.8 %copy.71 = f32[1280,3,384]{0,2,1:T(8,128)} copy(f32[1280,3,384]{2,0,1:T(8,128)} %mul.30) | data formatting | bytes 11796480 | tf_op jit(solution)/shard_map/mul | solution.py:54
  104.0 52.7 %convolution_bitcast_fusion = f32[2560,1152]{0,1:T(8,128)} fusion(f32[1280,1152]{0,1:T(8,128)} %bitcast.163, f32[2560,1280]{1,0:T(8,128)} %param.7), kind=kOutput, calls=%fused_computation | convolution fusion | flops 45298483200 | bytes 30801920 | tf_op jit(solution)/shard_map/dot_general | solution.py:13
  156.8 13.6 %copy.92 = f32[2560,1152]{1,0:T(8,128)} copy(f32[2560,1152]{0,1:T(8,128)} %convolution_bitcast_fusion) | data formatting | bytes 23592960
  171.1 6.0 %broadcast_in_dim.7 = f32[20,128,3,3,128]{1,0,4,3,2:T(8,128)} broadcast(f32[20,3,3]{0,2,1:T(4,128)S(1)} %convert_bitcast_fusion), dimensions={0,2,3} | broadcast | bytes 11797200 | tf_op jit(solution)/shard_map/broadcast_in_dim | solution.py:31
  177.1 13.7 %reshape.45 = f32[2560,3,384]{0,2,1:T(8,128)} reshape(f32[20,128,3,3,128]{1,0,4,3,2:T(8,128)} %broadcast_in_dim.7) | data formatting | bytes 23592960 | tf_op jit(solution)/shard_map/reshape | solution.py:32
  191.2 9.7 %mul.32 = f32[2560,3,384]{0,2,1:T(8,128)S(1)} multiply(f32[2560,3,384]{0,2,1:T(8,128)} %all-gather.5.cloned.1.call-done, f32[2560,3,384]{0,2,1:T(8,128)} %reshape.45) | non-fusion elementwise | flops 2949120 | bytes 35389440 | tf_op jit(solution)/shard_map/mul | solution.py:55
  200.9 4.3 copy-done
  205.3 50.1 %convolution_bitcast_fusion.1 = f32[1280,1152]{0,1:T(8,128)} fusion(f32[2560,1152]{0,1:T(8,128)S(1)} %bitcast.157, f32[2560,1280]{1,0:T(8,128)} %param.7), kind=kOutput, calls=%fused_computation.1 | convolution fusion | flops 45298483200 | bytes 30801920 | tf_op jit(solution)/shard_map/dot_general | solution.py:17
  255.4 7.7 %copy.94 = f32[1280,1152]{1,0:T(8,128)} copy(f32[1280,1152]{0,1:T(8,128)} %convolution_bitcast_fusion.1) | data formatting | bytes 11796480
  263.3 4.3 fusion.75
  267.6 9.3 %fusion.74 = (f32[2560,1,384]{0,2,1:T(8,128)}, f32[2560,1,384]{0,2,1:T(8,128)}, f32[2560,1,384]{0,2,1:T(8,128)}) fusion(f32[2560,3,384]{0,2,1:T(8,128)} %copy-done), kind=kLoop, calls=%fused_computation.100 | loop fusion | bytes 23592960 | tf_op jit(solution)/shard_map/slice | solution.py:72
  276.9 36.6 %reduce-scatter.7.cloned.1.call-done = f32[320,1152]{1,0:T(8,128)} async-done(((f32[2560,1152]{1,0:T(8,128)}), f32[320,1152]{1,0:T(8,128)}) %reduce-scatter.7.cloned.1.call-update) | async-done | bytes 1474576
  313.5 2.1 copy.93
  319.1 3.3 fusion.16
  323.5 3.3 fusion.18
  326.7 3.3 fusion.12
  331.9 3.2 fusion.14
  335.1 46.5 %reduce-scatter.9.cloned.1.call-done = f32[320,1152]{1,0:T(8,128)} async-done(((f32[1280,1152]{1,0:T(8,128)}), f32[320,1152]{1,0:T(8,128)}) %reduce-scatter.9.cloned.1.call-update) | async-done | bytes 1474576
  381.6 2.3 copy.95
  386.6 2.1 copy.100
  388.7 3.3 fusion.20
  393.1 3.2 fusion.49
  396.3 3.2 fusion.47
  402.5 2.2 pad_maximum_fusion
  407.0 137.7 %all-reduce.3.cloned.1.call-done = (f32[384,384]{1,0:T(8,128)}, f32[384,384]{1,0:T(8,128)}, f32[384,384]{1,0:T(8,128)}, f32[384,384]{1,0:T(8,128)}, f32[384,384]...) async-done(((f32[384,384]{1,0:T(8,128)}, f32[384,384]{1,0:T(8,128)}, f32[384,384]{1,0:T(8,128)}, f32[384,384]{1,0:T(8,128)}, f32[384,384]{1,0:T(8,128)}, ...) | async-done | bytes 4128784 | tf_op jit(solution)/shard_map/psum | solution.py:101
  546.3 2.5 fusion.7
  555.4 2.5 fusion.9
  (71 shorter events, 27.2 us)
Async XLA Ops:
  7.2 1.5 copy-start.16
  7.2 72.2 %all-gather.3.cloned.1.call-start = ((), (), s32[]{:S(2)}) async-start(), calls=%async_computation.2 | async-start | bytes 7372800 | tf_op jit(solution)/shard_map/all_gather | solution.py:54
  7.9 183.3 %all-gather.5.cloned.1.call-start = ((), (), s32[]{:S(2)}) async-start(), calls=%async_computation.3 | async-start | bytes 13271040 | tf_op jit(solution)/shard_map/all_gather | solution.py:55
  8.7 304.8 %reduce-scatter.7.cloned.1.call-start = ((), (), s32[]{:S(2)}) async-start(), calls=%async_computation.4 | async-start | bytes 13271040
  170.4 211.2 %reduce-scatter.9.cloned.1.call-start = ((), (), s32[]{:S(2)}) async-start(), calls=%async_computation.5 | async-start | bytes 7372800
  200.9 4.3 copy-start
  263.1 281.6 %all-reduce.3.cloned.1.call-start = ((), (), s32[]{:S(2)}) async-start(), calls=%async_computation.6 | async-start | bytes 8257536 | tf_op jit(solution)/shard_map/psum | solution.py:101
  317.8 4.5 copy-start.4
  319.1 3.3 copy-start.9
  331.1 0.8 copy-start.6
  385.2 6.8 %copy-start.1 = (f32[2,384,384]{2,1,0:T(8,128)S(1)}, f32[2,384,384]{2,1,0:T(8,128)}, u32[]{:S(2)}) copy-start(f32[2,384,384]{2,1,0:T(8,128)} %param.11) | copy-start | bytes 3538948
  388.7 3.3 copy-start.10
  400.4 2.1 copy-start.7
  404.7 1.1 copy-start.8
  544.7 1.5 copy-start.2
  544.7 1.6 copy-start.15
  544.7 4.2 copy-start.14
  546.1 2.7 copy-start.3
  546.1 2.7 copy-start.5
  548.8 1.3 copy-start.13
  550.1 1.3 copy-start.12
  551.5 1.6 copy-start.11
Sparse Core Ops, SparseCore 0:
  9.8 69.4 all-gather.2
  81.0 110.1 all-gather.4
  193.5 119.9 reduce-scatter.6
  316.4 65.2 reduce-scatter.8
  399.6 144.9 all-reduce.2
where the time goes:
time: 574 us; the launch traced here: 566 us
  waiting for transfers between devices  278 us (48%)
  matrix products  140 us (24%)
  local copies, waits for them, and re-layouts  105 us (18%)
  other arithmetic  26.1 us (5%)
  between operations  14.4 us (3%)
    psum x1, waiting for transfers between devices, per_device(): lax.psum(inner_product(upper_mine, inv_cols), ('row', 'col'))  138 us
    unnamed x7, waiting for transfers between devices  84.6 us
    dot_general x8, matrix products, inner_product(): lax.dot_general(left, right, (((0,), (0,)), ((), ())), precision=precise,...  72.9 us
    dot_general x9, matrix products, product(): jnp.dot(left, right, precision=precise, preferred_element_type=jnp.float32)  65.3 us
    all_gather x1, waiting for transfers between devices, per_device(): lax.all_gather(lower_anc, 'row', axis=2, tiled=True) * col_pattern  55.8 us
    unnamed x46, local copies, waits for them, and re-layouts  39.8 us
    reshape x2, local copies, waits for them, and re-layouts, tile_pattern(): return widened.reshape(blocks * BLK, SUPER, W)  24.2 us
  transfers between devices with their start and end apart: 5, of which 5 were waited for; matrix products, arithmetic and copies ran while one was open for 42% of the time, Pallas kernels for 0%

commit v1 on v0

--- a/solution.py
+++ b/solution.py
@@ -7,6 +7,11 @@
 BLK = 128
 SUPER = 3
 precise = lax.Precision.HIGHEST
+
+
+def axis_by_axis(array, one, other):
+    inner = lax.psum(array, one)
+    return lax.psum(inner, other)
 
 
 def product(left, right):
@@ -98,8 +103,8 @@
             inv_rows = inv_rows - outer_product(prev_rows, upper_side)
             cross_cols.append(cross_col)
             cross_rows.append(cross_row)
-        inv_corner = diag_inverse[node_index] - lax.psum(
-            inner_product(upper_mine, inv_cols), ("row", "col")
+        inv_corner = diag_inverse[node_index] - axis_by_axis(
+            inner_product(upper_mine, inv_cols), "col", "row"
         )
         if node_index > 0:
             inv_corner = inv_corner - product(upper_side, cross_col)

time: 574 us -> 703 us (1.22)
  waiting for transfers between devices: 278 us -> 402 us
    unnamed x7 -> x9, waiting for transfers between devices: 84.6 us -> 165 us
    psum x1 -> x3, waiting for transfers between devices: 138 us -> 180 us  [the longest x1 140 us: per_device(): rows_lower, upper_cols = lax.psum((rows_lower, upper_cols), ('row', 'col'))]
    unnamed x46 -> x44, local copies, waits for them, and re-layouts: 39.8 us -> 34.3 us
  transfers between devices with their start and end apart: 5 -> 7, of which waited for: 5 -> 7; matrix products, arithmetic and copies ran while one was open for 42% -> 35% of each run, Pallas kernels for 0% -> 0%
where the time goes in v1:
time: 703 us; the launch traced here: 695 us
  waiting for transfers between devices  402 us (57%)
  matrix products  146 us (21%)
  local copies, waits for them, and re-layouts  99.8 us (14%)
  other arithmetic  31.3 us (4%)
  between operations  14.7 us (2%)
    unnamed x9, waiting for transfers between devices  165 us
    psum x1, waiting for transfers between devices, per_device(): rows_lower, upper_cols = lax.psum((rows_lower, upper_cols), ('row', 'col'))  140 us
    dot_general x8, matrix products, inner_product(): lax.dot_general(left, right, (((0,), (0,)), ((), ())), precision=precise,...  75.9 us
    dot_general x9, matrix products, product(): jnp.dot(left, right, precision=precise, preferred_element_type=jnp.float32)  67.6 us
    all_gather x1, waiting for transfers between devices, per_device(): lax.all_gather(lower_anc, 'row', axis=2, tiled=True) * col_pattern  55.8 us
    psum x1, waiting for transfers between devices, axis_by_axis(): return lax.psum(inner, other)  39.1 us
    unnamed x44, local copies, waits for them, and re-layouts  34.3 us
    reshape x2, local copies, waits for them, and re-layouts, tile_pattern(): return widened.reshape(blocks * BLK, SUPER, W)  24.2 us
  transfers between devices with their start and end apart: 7, of which 7 were waited for; matrix products, arithmetic and copies ran while one was open for 35% of the time, Pallas kernels for 0%

profile of v1, /device:TPU:0, one launch (start us, length us, event | category | flops | bytes accessed | tf_op | source)
XLA Modules:
  0.0 694.6 jit_solution(81587714710747010)
XLA Ops:
  8.9 4.1 broadcast_in_dim.6
  13.0 10.5 %reshape.42 = f32[1280,3,384]{2,0,1:T(8,128)} reshape(f32[10,128,3,3,128]{4,3,1,0,2:T(4,128)} %broadcast_in_dim.6) | data formatting | bytes 11796480 | tf_op jit(solution)/shard_map/reshape | solution.py:37
  23.5 55.8 %all-gather.3.cloned.1.call-done = f32[1280,3,384]{0,2,1:T(8,128)} async-done(((f32[1280,3,96]{0,2,1:T(8,128)}), f32[1280,3,384]{0,2,1:T(8,128)}) %all-gather.3.cloned.1.call-update) | async-done | bytes 5898256 | tf_op jit(solution)/shard_map/all_gather | solution.py:59
  79.3 7.7 %copy.70 = f32[1280,3,384]{2,0,1:T(8,128)} copy(f32[1280,3,384]{0,2,1:T(8,128)} %all-gather.3.cloned.1.call-done) | data formatting | bytes 11796480 | tf_op jit(solution)/shard_map/all_gather | solution.py:59
  87.0 9.3 %mul.30 = f32[1280,3,384]{2,0,1:T(8,128)} multiply(f32[1280,3,384]{2,0,1:T(8,128)} %copy.70, f32[1280,3,384]{2,0,1:T(8,128)} %reshape.42) | non-fusion elementwise | flops 1474560 | bytes 17694720 | tf_op jit(solution)/shard_map/mul | solution.py:59
  96.3 7.8 %copy.71 = f32[1280,3,384]{0,2,1:T(8,128)} copy(f32[1280,3,384]{2,0,1:T(8,128)} %mul.30) | data formatting | bytes 11796480 | tf_op jit(solution)/shard_map/mul | solution.py:59
  104.1 52.7 %convolution_bitcast_fusion = f32[2560,1152]{0,1:T(8,128)} fusion(f32[1280,1152]{0,1:T(8,128)} %bitcast.163, f32[2560,1280]{1,0:T(8,128)} %param.7), kind=kOutput, calls=%fused_computation | convolution fusion | flops 45298483200 | bytes 30801920 | tf_op jit(solution)/shard_map/dot_general | solution.py:18
  156.7 13.5 %copy.92 = f32[2560,1152]{1,0:T(8,128)} copy(f32[2560,1152]{0,1:T(8,128)} %convolution_bitcast_fusion) | data formatting | bytes 23592960
  170.9 6.0 broadcast_in_dim.7
  177.0 13.7 %reshape.45 = f32[2560,3,384]{0,2,1:T(8,128)} reshape(f32[20,128,3,3,128]{1,0,4,3,2:T(8,128)} %broadcast_in_dim.7) | data formatting | bytes 23592960 | tf_op jit(solution)/shard_map/reshape | solution.py:37
  191.2 14.1 %mul.32 = f32[2560,3,384]{0,2,1:T(8,128)} multiply(f32[2560,3,384]{0,2,1:T(8,128)} %all-gather.5.cloned.1.call-done, f32[2560,3,384]{0,2,1:T(8,128)} %reshape.45) | non-fusion elementwise | flops 2949120 | bytes 35389440 | tf_op jit(solution)/shard_map/mul | solution.py:60
  205.3 9.1 %fusion.74 = (f32[2560,1,384]{0,2,1:T(8,128)}, f32[2560,1,384]{0,2,1:T(8,128)}, f32[2560,1,384]{0,2,1:T(8,128)}) fusion(f32[2560,3,384]{0,2,1:T(8,128)} %mul.32), kind=kLoop, calls=%fused_computation.100 | loop fusion | bytes 23592960 | tf_op jit(solution)/shard_map/slice | solution.py:77
  214.4 99.1 %reduce-scatter.7.cloned.1.call-done = f32[320,1152]{1,0:T(8,128)} async-done(((f32[2560,1152]{1,0:T(8,128)}), f32[320,1152]{1,0:T(8,128)}) %reduce-scatter.7.cloned.1.call-update) | async-done | bytes 1474576
  322.4 3.4 fusion.18
  325.8 3.2 fusion.20
  329.1 3.2 fusion.14
  332.5 52.9 %convolution_bitcast_fusion.1 = f32[1280,1152]{0,1:T(8,128)} fusion(f32[2560,1152]{0,1:T(8,128)} %bitcast.157, f32[2560,1280]{1,0:T(8,128)} %param.7), kind=kOutput, calls=%fused_computation.1 | convolution fusion | flops 45298483200 | bytes 30801920 | tf_op jit(solution)/shard_map/dot_general | solution.py:22
  385.4 7.7 %copy.94 = f32[1280,1152]{1,0:T(8,128)} copy(f32[1280,1152]{0,1:T(8,128)} %convolution_bitcast_fusion.1) | data formatting | bytes 11796480
  394.4 4.3 fusion.75
  398.7 64.9 %reduce-scatter.9.cloned.1.call-done = f32[320,1152]{1,0:T(8,128)} async-done(((f32[1280,1152]{1,0:T(8,128)}), f32[320,1152]{1,0:T(8,128)}) %reduce-scatter.9.cloned.1.call-update) | async-done | bytes 1474576
  463.6 2.3 copy.95
  469.3 3.3 fusion.12
  472.6 3.4 fusion.16
  476.0 3.2 fusion.49
  480.2 3.3 fusion.47
  487.3 2.3 pad_maximum_fusion
  491.9 39.1 %all-reduce.11.cloned.1.call-done = (f32[384,384]{1,0:T(8,128)}, f32[384,384]{1,0:T(8,128)}, f32[384,384]{1,0:T(8,128)}) async-done(((f32[384,384]{1,0:T(8,128)}, f32[384,384]{1,0:T(8,128)}, f32[384,384]{1,0:T(8,128)}), (f32[384,384]{1,0:T(8,128)}, f32[384,384]{1,0:T(8,128)}, f32[384,384]{1,0:T(8,128)})) %all-reduce.11.cloned.1.call-update) | async-done | bytes 1769488 | tf_op jit(solution)/shard_map/psum | solution.py:14
  531.0 2.2 fusion.73
  533.2 140.4 %all-reduce.7.cloned.1.call-done = (f32[384,384]{1,0:T(8,128)}, f32[384,384]{1,0:T(8,128)}, f32[384,384]{1,0:T(8,128)}, f32[384,384]{1,0:T(8,128)}) async-done(((f32[384,384]{1,0:T(8,128)}, f32[384,384]{1,0:T(8,128)}, f32[384,384]{1,0:T(8,128)}, f32[384,384]{1,0:T(8,128)}), (f32[384,384]{1,0:T(8,128)}, f32[384,384]{1,0:T(8,128)}, f32[384,384]{1,0:T(8,128)}, ...) | async-done | bytes 2359312 | tf_op jit(solution)/shard_map/psum | solution.py:98
  673.6 2.7 fusion.7
  676.3 2.4 fusion
  684.1 2.5 fusion.9
  (75 shorter events, 29.9 us)
Async XLA Ops:
  7.2 1.5 copy-start.15
  7.2 72.2 %all-gather.3.cloned.1.call-start = ((), (), s32[]{:S(2)}) async-start(), calls=%async_computation.2 | async-start | bytes 7372800 | tf_op jit(solution)/shard_map/all_gather | solution.py:59
  7.9 183.3 %all-gather.5.cloned.1.call-start = ((), (), s32[]{:S(2)}) async-start(), calls=%async_computation.3 | async-start | bytes 13271040 | tf_op jit(solution)/shard_map/all_gather | solution.py:60
  8.7 304.8 %reduce-scatter.7.cloned.1.call-start = ((), (), s32[]{:S(2)}) async-start(), calls=%async_computation.4 | async-start | bytes 13271040
  170.3 224.0 %all-reduce.9.cloned.1.call-start = ((), (), s32[]{:S(2)}) async-start(), calls=%async_computation.7 | async-start | bytes 3538944 | tf_op jit(solution)/shard_map/psum | solution.py:13
  316.6 2.6 copy-start.3
  322.4 6.7 copy-start.6
  332.3 131.2 %reduce-scatter.9.cloned.1.call-start = ((), (), s32[]{:S(2)}) async-start(), calls=%async_computation.5 | async-start | bytes 7372800
  393.2 137.8 %all-reduce.11.cloned.1.call-start = ((), (), s32[]{:S(2)}) async-start(), calls=%async_computation.8 | async-start | bytes 3538944 | tf_op jit(solution)/shard_map/psum | solution.py:14
  394.3 279.3 %all-reduce.7.cloned.1.call-start = ((), (), s32[]{:S(2)}) async-start(), calls=%async_computation.6 | async-start | bytes 4718592 | tf_op jit(solution)/shard_map/psum | solution.py:98
  472.6 6.5 copy-start
  472.6 6.5 copy-start.10
  484.3 3.0 copy-start.7
  487.3 2.3 copy-start.11
  489.6 1.1 copy-start.9
  531.0 142.6 %copy-start.1 = (f32[384,384]{1,0:T(8,128)S(1)}, f32[384,384]{1,0:T(8,128)}, u32[]{:S(2)}) copy-start(f32[384,384]{1,0:T(8,128)} %get-tuple-element.31) | copy-start | bytes 1769476
  533.2 143.1 %copy-start.4 = (f32[2,384,384]{2,1,0:T(8,128)S(1)}, f32[2,384,384]{2,1,0:T(8,128)}, u32[]{:S(2)}) copy-start(f32[2,384,384]{2,1,0:T(8,128)} %param.10) | copy-start | bytes 3538948
  673.6 2.7 copy-start.2
  676.3 2.4 copy-start.12
  678.7 1.6 copy-start.14
  680.3 1.3 copy-start.5
  680.3 1.4 copy-start.13
  683.4 3.3 copy-start.8
Sparse Core Ops, SparseCore 0:
  9.8 69.4 all-gather.2
  81.0 110.1 all-gather.4
  193.5 119.9 reduce-scatter.6
  332.4 61.7 all-reduce.8
  397.1 66.3 reduce-scatter.8
  466.9 64.1 all-reduce.10
  537.0 136.5 all-reduce.6
